TPU v7x, 256 devices: a whole 4x4x8 slice. The times are simulated.
256 devices in a mesh: dp: 8 (over x, core), group: 32 (over z, y).
Axes of the slice: x: 4, y: 4, z: 8, core: 2. Of those that a mesh axis runs over, the one named last changes fastest.
Arguments:
- embeds: bfloat16 [65536, 1024], P(('dp', 'group')), may hold values from -6 to 6
- row_ids: int32 [65536], P(('dp', 'group')), may hold values from 0 to 63
- neighbors: int32 [256, 3], P('dp'), may hold values from 0 to 31, as said below
- w_first: bfloat16 [1024, 4096], P(None, 'dp'), may hold values from -0.1875 to 0.1875
- w_second: bfloat16 [4096, 1024], P('dp'), may hold values from -0.09375 to 0.09375
Outputs:
- grad_first: float32 [1024, 4096], P('group', 'dp')
- grad_second: float32 [4096, 1024], P('dp', 'group')
- grad_unit: float32 [65536, 1024], P(('dp', 'group'))
Inputs may be any that keep to these rules, and one draw needn't show every extreme that they name: `neighbors`: within a row the 3 entries differ from one another and from the row's own index b % 32.
All inputs are finite; a program needn't handle non-finite values.
Results may differ from a plain program's by a relative error of at most 0.013.
Values may be sent and summed in bfloat16 or wider, within the bound.
No kernel may reach another device: no remote copies, remote signals or barrier semaphores. Data moves between devices by JAX's collectives and lax.ppermute only.
A program may use at most 64 MiB of HBM per device.

v0:
```python
import jax
import jax.numpy as jnp
from jax import lax
from jax.sharding import PartitionSpec as P

EPS = 1e-06
TEMP = 10.0
SHIFT = -5.0


def gelu_fwd(value):
    return jax.nn.gelu(value, approximate=True)


def gelu_back(pre, grad):
    _, back = jax.vjp(gelu_fwd, pre)
    return back(grad)[0]


def per_device(embeds, row_ids, neighbors, w_first, w_second):
    owners = lax.axis_size("group")
    block = embeds.shape[0]
    piece = block // owners
    width = w_second.shape[1]
    listed = neighbors.shape[1]
    gathered = lax.all_gather(embeds, "dp", axis=0, tiled=True)
    pre = jnp.dot(gathered, w_first, preferred_element_type=jnp.float32)
    hidden = gelu_fwd(pre).astype(jnp.bfloat16)
    proj = lax.psum_scatter(
        jnp.dot(hidden, w_second, preferred_element_type=jnp.float32).astype(jnp.bfloat16),
        "dp",
        scatter_dimension=0,
        tiled=True,
    ).astype(jnp.float32)
    inv = lax.rsqrt(jnp.mean(proj * proj, axis=-1, keepdims=True) + EPS)
    unit = proj * inv
    unit_b = unit.astype(jnp.bfloat16)
    held, held_ids = (
        lax.all_to_all(
            unit_b.reshape(owners, piece, width), "group", split_axis=0, concat_axis=0, tiled=True
        ),
        lax.all_to_all(
            row_ids.reshape(owners, piece), "group", split_axis=0, concat_axis=0, tiled=True
        ),
    )
    order = neighbors.T
    outgoing = jnp.take(held, order, axis=0)
    outgoing_ids = jnp.take(held_ids, order, axis=0)
    fetched, fetched_ids = (
        lax.all_to_all(outgoing, "group", split_axis=1, concat_axis=1, tiled=True),
        lax.all_to_all(outgoing_ids, "group", split_axis=1, concat_axis=1, tiled=True),
    )
    cand = jnp.concatenate([unit_b[None], fetched.reshape(listed, block, width)], 0)
    cand_ids = jnp.concatenate([row_ids[None], fetched_ids.reshape(listed, block)], 0)
    logits = (
        TEMP / width * jnp.einsum("rp,kcp->krc", unit_b, cand, preferred_element_type=jnp.float32)
        + SHIFT
    )
    sign = jnp.where(row_ids[None, :, None] == cand_ids[:, None, :], 1.0, -1.0).astype(jnp.float32)
    weight = (-sign * jax.nn.sigmoid(-sign * logits) * (TEMP / width)).astype(jnp.bfloat16)
    grad_own = jnp.einsum("krc,kcp->rp", weight, cand, preferred_element_type=jnp.float32)
    grad_cand = jnp.einsum("krc,rp->kcp", weight, unit_b, preferred_element_type=jnp.float32)
    returned = lax.all_to_all(
        grad_cand[1:].reshape(listed, owners, piece, width),
        "group",
        split_axis=1,
        concat_axis=1,
        tiled=True,
    )
    select = (order[:, :, None] == jnp.arange(owners, dtype=jnp.int32)[None, None, :]).astype(
        jnp.float32
    )
    summed = jnp.einsum("krb,krqp->bqp", select, returned, precision=lax.Precision.HIGHEST)
    collected = lax.all_to_all(summed, "group", split_axis=0, concat_axis=0, tiled=True)
    grad_unit = grad_own + grad_cand[0] + collected.reshape(block, width)
    grad_proj = inv * (grad_unit - unit * jnp.mean(unit * grad_unit, axis=-1, keepdims=True))
    grad_all = lax.all_gather(grad_proj.astype(jnp.bfloat16), "dp", axis=0, tiled=True)
    second_local = lax.dot_general(
        hidden, grad_all, (((0,), (0,)), ((), ())), preferred_element_type=jnp.float32
    )
    grad_hidden = lax.dot_general(
        grad_all, w_second, (((1,), (1,)), ((), ())), preferred_element_type=jnp.float32
    )
    grad_pre = gelu_back(pre, grad_hidden).astype(jnp.bfloat16)
    first_local = lax.dot_general(
        gathered, grad_pre, (((0,), (0,)), ((), ())), preferred_element_type=jnp.float32
    )
    first_out, second_out = (
        lax.psum_scatter(first_local, "group", scatter_dimension=0, tiled=True),
        lax.psum_scatter(second_local, "group", scatter_dimension=1, tiled=True),
    )
    return (first_out, second_out, grad_unit)


def solution(mesh):
    in_specs = (
        P(("dp", "group"), None),
        P(("dp", "group")),
        P("dp", None),
        P(None, "dp"),
        P("dp", None),
    )
    out_specs = (P("group", "dp"), P("dp", "group"), P(("dp", "group"), None))
    return jax.shard_map(
        per_device, mesh=mesh, in_specs=in_specs, out_specs=out_specs, check_vma=False
    )
```

profile of v0, /device:TPU:4, one launch (start us, length us, event | category | flops | bytes accessed | tf_op | source)
XLA Modules:
  0.0 792.0 jit_solution(12244141082356973376)
XLA Ops:
  8.0 38.2 %all-gather.3.cloned.1.call-done = bf16[2048,1024]{1,0:T(8,128)(2,1)} async-done(((bf16[256,1024]{1,0:T(8,128)(2,1)}), bf16[2048,1024]{1,0:T(8,128)(2,1)}) %all-gather.3.cloned.1.call-update) | async-done | bytes 4194320 | tf_op jit(solution)/shard_map/all_gather | solution.py:26
  46.2 4.8 fusion.58
  51.0 2.0 copy-done.6
  53.0 4.8 convolution_convert_fusion
  59.1 9.9 %all-to-all-start = ((s32[32,1,8]{2,1,0:T(1,128)}), s32[32,1,8]{2,1,0:T(1,128)S(1)}, u32[]{:S(2)}, u32[]{:S(2)}) async-start(s32[32,1,8]{2,1,0:T(1,128)} %bitcast.2), calls=%async_computation.1 | async-start | bytes 32768 | tf_op jit(solution)/shard_map/all_to_all | solution.py:42
  69.0 26.2 %reduce-scatter.6.cloned.1.call-done = bf16[256,1024]{1,0:T(8,128)(2,1)} async-done(((bf16[2048,1024]{1,0:T(8,128)(2,1)}), bf16[256,1024]{1,0:T(8,128)(2,1)}) %reduce-scatter.6.cloned.1.call-update) | async-done | bytes 524304 | tf_op jit(solution)/shard_map/reduce_scatter | solution.py:29
  96.4 2.2 fusion.54
  98.6 9.6 %all-to-all-start.2 = ((bf16[32,8,1024]{2,1,0:T(8,128)(2,1)}), bf16[32,8,1024]{2,1,0:T(8,128)(2,1)S(1)}, u32[]{:S(2)}, u32[]{:S(2)}) async-start(bf16[32,8,1024]{2,1,0:T(8,128)(2,1)} %get-tuple-element.19), calls=%async_computation.3 | async-start | bytes 1048576 | tf_op jit(solution)/shard_map/all_to_all | solution.py:39
  109.8 16.9 %all-to-all-done.2 = bf16[32,8,1024]{2,1,0:T(8,128)(2,1)S(1)} async-done(((bf16[32,8,1024]{2,1,0:T(8,128)(2,1)}), bf16[32,8,1024]{2,1,0:T(8,128)(2,1)S(1)}, u32[]{:S(2)}, u32[]{:S(2)}) %all-to-all-start.2) | async-done | bytes 524320 | tf_op jit(solution)/shard_map/all_to_all | solution.py:39
  126.8 4.7 all-to-all-start.1
  132.4 1.3 copy.46
  133.8 7.7 all-to-all-done.1
  141.5 4.0 all-to-all-start.3
  145.6 37.7 %all-to-all-done.3 = bf16[3,32,8,1024]{3,2,0,1:T(8,128)(2,1)S(1)} async-done(((bf16[3,32,8,1024]{3,2,0,1:T(8,128)(2,1)}), bf16[3,32,8,1024]{3,2,0,1:T(8,128)(2,1)S(1)}, u32[]{:S(2)}, u32[]{:S(2)}) %all-to-all-start.3) | async-done | bytes 1572896 | tf_op jit(solution)/shard_map/all_to_all | solution.py:50
  183.5 2.1 fusion.31
  187.2 75.9 %all_to_all.37 = f32[3,32,8,1024]{3,2,0,1:T(8,128)S(1)} all-to-all(f32[3,32,8,1024]{3,2,0,1:T(8,128)S(1)} %copy.50), channel_id=1, replica_groups=mesh['dp'=8,'group'=32] {'group'}, dimensions={1} | all-to-all | bytes 6291456 | tf_op jit(solution)/shard_map/all_to_all | solution.py:63
  263.2 3.1 fusion.14
  266.9 31.0 %all_to_all.38 = f32[32,8,1024]{2,1,0:T(8,128)S(1)} all-to-all(f32[32,8,1024]{2,1,0:T(8,128)S(1)} %copy.52), channel_id=1, replica_groups=mesh['dp'=8,'group'=32] {'group'}, dimensions={0} | all-to-all | bytes 2097152 | tf_op jit(solution)/shard_map/all_to_all | solution.py:74
  300.9 33.7 %all-gather.5.cloned.1.call-done = bf16[2048,1024]{1,0:T(8,128)(2,1)} async-done(((bf16[256,1024]{1,0:T(8,128)(2,1)}), bf16[2048,1024]{1,0:T(8,128)(2,1)}) %all-gather.5.cloned.1.call-update) | async-done | bytes 4194320 | tf_op jit(solution)/shard_map/all_gather | solution.py:77
  334.6 11.6 %fusion.11 = f32[1024,512]{0,1:T(8,128)S(1)} fusion(bf16[2048,1024]{1,0:T(8,128)(2,1)} %all-gather.3.cloned.1.call-done, f32[2048,512]{1,0:T(8,128)} %copy-done.6, bf16[2048,1024]{1,0:T(8,128)(2,1)} %all-gather.5.cloned.1.call-done, bf16[512,1024]{1,0:T(8,128)(2,1)S(1)} %copy-done), kind=kOutput, calls=%fused_computation.18 | convolution fusion | flops 4315938816 | bytes 15728640 | tf_op jit(solution)/shard_map/dot_general | solution.py:85
  346.2 1.9 copy.56
  348.1 7.3 fusion.55
  355.5 210.5 %reduce-scatter.10.cloned.1.call-done = f32[32,512]{1,0:T(8,128)} async-done(((f32[1024,512]{1,0:T(8,128)}), f32[32,512]{1,0:T(8,128)}) %reduce-scatter.10.cloned.1.call-update) | async-done | bytes 65552
  566.0 219.4 %reduce-scatter.8.cloned.1.call-done = f32[512,32]{0,1:T(8,128)} async-done(((f32[512,1024]{0,1:T(8,128)}), f32[512,32]{0,1:T(8,128)}) %reduce-scatter.8.cloned.1.call-update) | async-done | bytes 65552 | tf_op jit(solution)/shard_map/reduce_scatter | solution.py:90
  (47 shorter events, 11.5 us)
Async XLA Ops:
  7.2 45.8 %copy-start = (bf16[512,1024]{1,0:T(8,128)(2,1)S(1)}, bf16[512,1024]{1,0:T(8,128)(2,1)}, u32[]{:S(2)}) copy-start(bf16[512,1024]{1,0:T(8,128)(2,1)} %param.9) | copy-start | bytes 3145732
  7.2 39.0 %all-gather.3.cloned.1.call-start = ((), (), s32[]{:S(2)}) async-start(), calls=%async_computation.9 | async-start | bytes 4718592 | tf_op jit(solution)/shard_map/all_gather | solution.py:26
  7.9 87.3 %reduce-scatter.6.cloned.1.call-start = ((), (), s32[]{:S(2)}) async-start(), calls=%async_computation.10 | async-start | bytes 4718592 | tf_op jit(solution)/shard_map/reduce_scatter | solution.py:29
  51.0 2.0 copy-start.6
  57.8 0.7 copy-start.5
  57.8 50.5 %copy-start.4 = (s32[32,3]{0,1:T(4,128)S(1)}, s32[32,3]{0,1:T(4,128)}, u32[]{:S(2)}) copy-start(s32[32,3]{0,1:T(4,128)} %param.7) | copy-start | bytes 1156
  59.1 39.5 %all-to-all-start = ((s32[32,1,8]{2,1,0:T(1,128)}), s32[32,1,8]{2,1,0:T(1,128)S(1)}, u32[]{:S(2)}, u32[]{:S(2)}) async-start(s32[32,1,8]{2,1,0:T(1,128)} %bitcast.2), calls=%async_computation.1 | async-start | bytes 32768 | tf_op jit(solution)/shard_map/all_to_all | solution.py:42
  98.6 28.1 %all-to-all-start.2 = ((bf16[32,8,1024]{2,1,0:T(8,128)(2,1)}), bf16[32,8,1024]{2,1,0:T(8,128)(2,1)S(1)}, u32[]{:S(2)}, u32[]{:S(2)}) async-start(bf16[32,8,1024]{2,1,0:T(8,128)(2,1)} %get-tuple-element.19), calls=%async_computation.3 | async-start | bytes 1048576 | tf_op jit(solution)/shard_map/all_to_all | solution.py:39
  126.8 14.7 %all-to-all-start.1 = ((s32[3,32,8]{2,0,1:T(4,128)}), s32[3,32,8]{2,0,1:T(4,128)S(1)}, u32[]{:S(2)}, u32[]{:S(2)}) async-start(s32[3,32,8]{2,0,1:T(4,128)} %copy_select_fusion), calls=%async_computation.2 | async-start | bytes 131072 | tf_op jit(solution)/shard_map/all_to_all | solution.py:51
  132.4 51.0 %copy-start.1 = (bf16[256,1024]{1,0:T(8,128)(2,1)S(1)}, bf16[256,1024]{1,0:T(8,128)(2,1)}, u32[]{:S(2)}) copy-start(bf16[256,1024]{1,0:T(8,128)(2,1)} %reduce-scatter.6.cloned.1.call-done) | copy-start | bytes 1572868
  141.5 41.9 %all-to-all-start.3 = ((bf16[3,32,8,1024]{3,2,0,1:T(8,128)(2,1)}), bf16[3,32,8,1024]{3,2,0,1:T(8,128)(2,1)S(1)}, u32[]{:S(2)}, u32[]{:S(2)}) async-start(bf16[3,32,8,1024]{3,2,0,1:T(8,128)(2,1)} %copy.46), calls=%async_computation.4 | async-start | bytes 3145728 | tf_op jit(solution)/shard_map/all_to_all | solution.py:50
  145.5 189.2 %all-gather.5.cloned.1.call-start = ((), (), s32[]{:S(2)}) async-start(), calls=%async_computation.11 | async-start | bytes 4718592 | tf_op jit(solution)/shard_map/all_gather | solution.py:77
  263.2 34.7 %copy-start.3 = (bf16[1,256,1024]{2,1,0:T(8,128)(2,1)S(1)}, bf16[1,256,1024]{2,1,0:T(8,128)(2,1)}, u32[]{:S(2)}) copy-start(bf16[1,256,1024]{2,1,0:T(8,128)(2,1)} %get-tuple-element.18) | copy-start | bytes 1572868
  298.8 1.0 copy-start.2
  300.9 265.1 %reduce-scatter.10.cloned.1.call-start = ((), (), s32[]{:S(2)}) async-start(), calls=%async_computation.13 | async-start | bytes 2162688
  348.1 437.3 %reduce-scatter.8.cloned.1.call-start = ((), (), s32[]{:S(2)}) async-start(), calls=%async_computation.12 | async-start | bytes 2162688 | tf_op jit(solution)/shard_map/reduce_scatter | solution.py:90
Sparse Core Ops, SparseCore 0:
  9.9 36.2 all-gather.2
  57.9 37.2 reduce-scatter.5
  301.0 33.5 all-gather.4
  348.2 217.7 reduce-scatter.9
  570.7 214.6 reduce-scatter.7
where the time goes:
time: 793 us; the launch traced here: 792 us
  waiting for transfers between devices  591 us (75%)
  blocking collectives  107 us (13%)
  matrix products  35.4 us (4%)
  starting transfers between devices  28.3 us (4%)
  between operations  14 us (2%)
  local copies, waits for them, and re-layouts  10.6 us (1%)
    reduce_scatter x1, waiting for transfers between devices, per_device(): lax.psum_scatter(second_local, 'group', scatter_dimension=1, tiled=True)  219 us
    unnamed x6, waiting for transfers between devices  211 us
    all_to_all x1, blocking collectives, per_device(): lax.all_to_all(grad_cand[1:].reshape(listed, owners, piece, width), 'grou...  75.9 us
    all_gather x1, waiting for transfers between devices, per_device(): gathered = lax.all_gather(embeds, 'dp', axis=0, tiled=True)  38.2 us
    all_to_all x1, waiting for transfers between devices, per_device(): lax.all_to_all(outgoing, 'group', split_axis=1, concat_axis=1, tiled=True)  37.7 us
    all_gather x1, waiting for transfers between devices, per_device(): lax.all_gather(grad_proj.astype(jnp.bfloat16), 'dp', axis=0, tiled=True)  33.7 us
    all_to_all x1, blocking collectives, per_device(): lax.all_to_all(summed, 'group', split_axis=0, concat_axis=0, tiled=True)  31 us
    reduce_scatter x1, waiting for transfers between devices, per_device(): lax.psum_scatter(jnp.dot(hidden, w_second, preferred_element_type=jnp.flo...  26.2 us
  transfers between devices with their start and end apart: 9, of which 8 were waited for; matrix products, arithmetic and copies ran while one was open for 2% of the time, Pallas kernels for 0%

commit v1 on v0

--- a/solution.py
+++ b/solution.py
@@ -1,11 +1,27 @@
+import functools
 import jax
 import jax.numpy as jnp
 from jax import lax
 from jax.sharding import PartitionSpec as P
+from jax.lax import all_to_all, axis_size
 
 EPS = 1e-06
 TEMP = 10.0
 SHIFT = -5.0
+
+
+def proceed_clusters_on(u, peer_axis, axis_k, dim_k):
+    formed = all_to_all(
+        jnp.stack(jnp.split(u, axis_size(peer_axis), axis_k), axis=0),
+        axis_name=peer_axis,
+        split_axis=0,
+        concat_axis=0,
+    )
+    low = jnp.concatenate(formed, axis=dim_k)
+    return low
+
+
+_build_task = functools.partial(proceed_clusters_on, peer_axis="group", axis_k=1, dim_k=1)
 
 
 def gelu_fwd(value):
@@ -47,7 +63,7 @@
     outgoing = jnp.take(held, order, axis=0)
     outgoing_ids = jnp.take(held_ids, order, axis=0)
     fetched, fetched_ids = (
-        lax.all_to_all(outgoing, "group", split_axis=1, concat_axis=1, tiled=True),
+        _build_task(outgoing),
         lax.all_to_all(outgoing_ids, "group", split_axis=1, concat_axis=1, tiled=True),
     )
     cand = jnp.concatenate([unit_b[None], fetched.reshape(listed, block, width)], 0)

time: 793 us -> 792 us (level)
  no operation moved by 1% of the time
where the time goes in v1:
time: 792 us
  waiting for transfers between devices  591 us (75%)
  blocking collectives  107 us (14%)
  matrix products  34.4 us (4%)
  starting transfers between devices  28.6 us (4%)
  between operations  14.2 us (2%)
  local copies, waits for them, and re-layouts  11.6 us (1%)
    reduce_scatter x1, waiting for transfers between devices, per_device(): lax.psum_scatter(second_local, 'group', scatter_dimension=1, tiled=True)  219 us
    unnamed x6, waiting for transfers between devices  211 us
    all_to_all x1, blocking collectives, per_device(): lax.all_to_all(grad_cand[1:].reshape(listed, owners, piece, width), 'grou...  75.9 us
    all_gather x1, waiting for transfers between devices, per_device(): gathered = lax.all_gather(embeds, 'dp', axis=0, tiled=True)  38.2 us
    all_to_all x1, waiting for transfers between devices, proceed_clusters_on(): all_to_all(jnp.stack(jnp.split(u, axis_size(peer_axis), axis_k), axis=0),...  37.7 us
    all_gather x1, waiting for transfers between devices, per_device(): lax.all_gather(grad_proj.astype(jnp.bfloat16), 'dp', axis=0, tiled=True)  33.8 us
    all_to_all x1, blocking collectives, per_device(): lax.all_to_all(summed, 'group', split_axis=0, concat_axis=0, tiled=True)  31 us
    reduce_scatter x1, waiting for transfers between devices, per_device(): lax.psum_scatter(jnp.dot(hidden, w_second, preferred_element_type=jnp.flo...  26 us
  transfers between devices with their start and end apart: 9, of which 8 were waited for; matrix products, arithmetic and copies ran while one was open for 2% of the time, Pallas kernels for 0%

profile of v1, /device:TPU:4, one launch (start us, length us, event | category | flops | bytes accessed | tf_op | source)
XLA Modules:
  0.0 791.8 jit_solution(4479436548519203982)
XLA Ops:
  8.0 38.2 %all-gather.3.cloned.1.call-done = bf16[2048,1024]{1,0:T(8,128)(2,1)} async-done(((bf16[256,1024]{1,0:T(8,128)(2,1)}), bf16[2048,1024]{1,0:T(8,128)(2,1)}) %all-gather.3.cloned.1.call-update) | async-done | bytes 4194320 | tf_op jit(solution)/shard_map/all_gather | solution.py:42
  46.2 4.8 fusion.58
  51.0 1.9 copy-done.7
  53.0 4.8 convolution_convert_fusion
  59.1 9.8 %all-to-all-start = ((s32[32,1,8]{2,1,0:T(1,128)}), s32[32,1,8]{2,1,0:T(1,128)S(1)}, u32[]{:S(2)}, u32[]{:S(2)}) async-start(s32[32,1,8]{2,1,0:T(1,128)} %bitcast.2), calls=%async_computation.1 | async-start | bytes 32768 | tf_op jit(solution)/shard_map/all_to_all | solution.py:58
  69.0 26.0 %reduce-scatter.6.cloned.1.call-done = bf16[256,1024]{1,0:T(8,128)(2,1)} async-done(((bf16[2048,1024]{1,0:T(8,128)(2,1)}), bf16[256,1024]{1,0:T(8,128)(2,1)}) %reduce-scatter.6.cloned.1.call-update) | async-done | bytes 524304 | tf_op jit(solution)/shard_map/reduce_scatter | solution.py:45
  95.0 1.2 fusion.36
  96.3 2.2 fusion.54
  98.5 9.7 %all-to-all-start.2 = ((bf16[32,8,1024]{2,1,0:T(8,128)(2,1)}), bf16[32,8,1024]{2,1,0:T(8,128)(2,1)S(1)}, u32[]{:S(2)}, u32[]{:S(2)}) async-start(bf16[32,8,1024]{2,1,0:T(8,128)(2,1)} %get-tuple-element.19), calls=%async_computation.3 | async-start | bytes 1048576 | tf_op jit(solution)/shard_map/all_to_all | solution.py:55
  109.8 16.8 %all-to-all-done.2 = bf16[32,8,1024]{2,1,0:T(8,128)(2,1)S(1)} async-done(((bf16[32,8,1024]{2,1,0:T(8,128)(2,1)}), bf16[32,8,1024]{2,1,0:T(8,128)(2,1)S(1)}, u32[]{:S(2)}, u32[]{:S(2)}) %all-to-all-start.2) | async-done | bytes 524320 | tf_op jit(solution)/shard_map/all_to_all | solution.py:55
  126.6 4.9 all-to-all-start.1
  132.9 1.2 copy-done.2
  134.1 7.4 all-to-all-done.1
  141.5 4.0 all-to-all-start.3
  145.6 37.7 %all-to-all-done.3 = bf16[32,3,1,8,1024]{4,3,1,2,0:T(8,128)(2,1)S(1)} async-done(((bf16[32,3,1,8,1024]{4,3,1,2,0:T(8,128)(2,1)}), bf16[32,3,1,8,1024]{4,3,1,2,0:T(8,128)(2,1)S(1)}, u32[]{:S(2)}, u32[]{:S(2)}) %all-to-all-start.3) | async-done | bytes 1572896 | tf_op jit(solution)/shard_map/all_to_all | solution.py:14
  187.1 75.9 %all_to_all.37 = f32[3,32,8,1024]{3,2,0,1:T(8,128)S(1)} all-to-all(f32[3,32,8,1024]{3,2,0,1:T(8,128)S(1)} %copy.176), channel_id=1, replica_groups=mesh['dp'=8,'group'=32] {'group'}, dimensions={1} | all-to-all | bytes 6291456 | tf_op jit(solution)/shard_map/all_to_all | solution.py:79
  263.0 3.1 fusion.14
  266.7 31.0 %all_to_all.38 = f32[32,8,1024]{2,1,0:T(8,128)S(1)} all-to-all(f32[32,8,1024]{2,1,0:T(8,128)S(1)} %copy.178), channel_id=1, replica_groups=mesh['dp'=8,'group'=32] {'group'}, dimensions={0} | all-to-all | bytes 2097152 | tf_op jit(solution)/shard_map/all_to_all | solution.py:90
  300.8 33.8 %all-gather.5.cloned.1.call-done = bf16[2048,1024]{1,0:T(8,128)(2,1)} async-done(((bf16[256,1024]{1,0:T(8,128)(2,1)}), bf16[2048,1024]{1,0:T(8,128)(2,1)}) %all-gather.5.cloned.1.call-update) | async-done | bytes 4194320 | tf_op jit(solution)/shard_map/all_gather | solution.py:93
  334.6 11.6 %fusion.11 = f32[1024,512]{0,1:T(8,128)S(1)} fusion(bf16[2048,1024]{1,0:T(8,128)(2,1)} %all-gather.3.cloned.1.call-done, f32[2048,512]{1,0:T(8,128)} %copy-done.7, bf16[2048,1024]{1,0:T(8,128)(2,1)} %all-gather.5.cloned.1.call-done, bf16[512,1024]{1,0:T(8,128)(2,1)S(1)} %copy-done), kind=kOutput, calls=%fused_computation.18 | convolution fusion | flops 4315938816 | bytes 15728640 | tf_op jit(solution)/shard_map/dot_general | solution.py:101
  346.2 1.9 copy.182
  348.2 7.3 fusion.55
  355.5 210.4 %reduce-scatter.10.cloned.1.call-done = f32[32,512]{1,0:T(8,128)} async-done(((f32[1024,512]{1,0:T(8,128)}), f32[32,512]{1,0:T(8,128)}) %reduce-scatter.10.cloned.1.call-update) | async-done | bytes 65552
  565.9 219.3 %reduce-scatter.8.cloned.1.call-done = f32[512,32]{0,1:T(8,128)} async-done(((f32[512,1024]{0,1:T(8,128)}), f32[512,32]{0,1:T(8,128)}) %reduce-scatter.8.cloned.1.call-update) | async-done | bytes 65552 | tf_op jit(solution)/shard_map/reduce_scatter | solution.py:106
  (80 shorter events, 12.4 us)
Async XLA Ops:
  7.2 45.8 %copy-start = (bf16[512,1024]{1,0:T(8,128)(2,1)S(1)}, bf16[512,1024]{1,0:T(8,128)(2,1)}, u32[]{:S(2)}) copy-start(bf16[512,1024]{1,0:T(8,128)(2,1)} %param.9) | copy-start | bytes 3145732
  7.2 39.0 %all-gather.3.cloned.1.call-start = ((), (), s32[]{:S(2)}) async-start(), calls=%async_computation.9 | async-start | bytes 4718592 | tf_op jit(solution)/shard_map/all_gather | solution.py:42
  7.9 87.1 %reduce-scatter.6.cloned.1.call-start = ((), (), s32[]{:S(2)}) async-start(), calls=%async_computation.10 | async-start | bytes 4718592 | tf_op jit(solution)/shard_map/reduce_scatter | solution.py:45
  51.0 2.0 copy-start.7
  57.7 0.7 copy-start.6
  59.1 39.4 %all-to-all-start = ((s32[32,1,8]{2,1,0:T(1,128)}), s32[32,1,8]{2,1,0:T(1,128)S(1)}, u32[]{:S(2)}, u32[]{:S(2)}) async-start(s32[32,1,8]{2,1,0:T(1,128)} %bitcast.2), calls=%async_computation.1 | async-start | bytes 32768 | tf_op jit(solution)/shard_map/all_to_all | solution.py:58
  69.0 39.2 %copy-start.5 = (s32[32,3]{0,1:T(4,128)S(1)}, s32[32,3]{0,1:T(4,128)}, u32[]{:S(2)}) copy-start(s32[32,3]{0,1:T(4,128)} %param.7) | copy-start | bytes 1156
  98.5 28.1 %all-to-all-start.2 = ((bf16[32,8,1024]{2,1,0:T(8,128)(2,1)}), bf16[32,8,1024]{2,1,0:T(8,128)(2,1)S(1)}, u32[]{:S(2)}, u32[]{:S(2)}) async-start(bf16[32,8,1024]{2,1,0:T(8,128)(2,1)} %get-tuple-element.19), calls=%async_computation.3 | async-start | bytes 1048576 | tf_op jit(solution)/shard_map/all_to_all | solution.py:55
  126.6 14.9 %all-to-all-start.1 = ((s32[3,32,8]{2,0,1:T(4,128)}), s32[3,32,8]{2,0,1:T(4,128)S(1)}, u32[]{:S(2)}, u32[]{:S(2)}) async-start(s32[3,32,8]{2,0,1:T(4,128)} %copy_select_fusion), calls=%async_computation.2 | async-start | bytes 131072 | tf_op jit(solution)/shard_map/all_to_all | solution.py:67
  132.9 1.2 copy-start.2
  141.5 41.9 %all-to-all-start.3 = ((bf16[32,3,1,8,1024]{4,3,1,2,0:T(8,128)(2,1)}), bf16[32,3,1,8,1024]{4,3,1,2,0:T(8,128)(2,1)S(1)}, u32[]{:S(2)}, u32[]{:S(2)}) async-start(bf16[32,3,1,8,1024]{4,3,1,2,0:T(8,128)(2,1)} %copy-done.2), calls=%async_computation.4 | async-start | bytes 3145728 | tf_op jit(solution)/shard_map/all_to_all | solution.py:14
  145.4 189.2 %all-gather.5.cloned.1.call-start = ((), (), s32[]{:S(2)}) async-start(), calls=%async_computation.11 | async-start | bytes 4718592 | tf_op jit(solution)/shard_map/all_gather | solution.py:93
  145.6 37.9 %copy-start.1 = (bf16[256,1024]{1,0:T(8,128)(2,1)S(1)}, bf16[256,1024]{1,0:T(8,128)(2,1)}, u32[]{:S(2)}) copy-start(bf16[256,1024]{1,0:T(8,128)(2,1)} %reduce-scatter.6.cloned.1.call-done) | copy-start | bytes 1572868
  183.3 1.0 copy-start.4
  298.6 1.0 copy-start.3
  300.7 265.2 %reduce-scatter.10.cloned.1.call-start = ((), (), s32[]{:S(2)}) async-start(), calls=%async_computation.13 | async-start | bytes 2162688
  348.1 437.1 %reduce-scatter.8.cloned.1.call-start = ((), (), s32[]{:S(2)}) async-start(), calls=%async_computation.12 | async-start | bytes 2162688 | tf_op jit(solution)/shard_map/reduce_scatter | solution.py:106
Sparse Core Ops, SparseCore 0:
  9.9 36.2 all-gather.2
  57.9 37.0 reduce-scatter.5
  300.9 33.7 all-gather.4
  348.2 217.6 reduce-scatter.9
  570.6 214.5 reduce-scatter.7
